TPU v7x, 512 devices: a whole 4x4x16 slice. The times are simulated.
512 devices in a mesh: sect: 4 (over y), blk: 128 (over x, z, core).
Axes of the slice: x: 4, y: 4, z: 16, core: 2. Of those that a mesh axis runs over, the one named last changes fastest.
Arguments:
- site_tensor: bfloat16 [4, 6144, 1536], P('sect', 'blk'), may hold values from -0.5 to 0.5
- left_env: bfloat16 [4, 256, 384, 384], P('sect', 'blk'), may hold values from -0.23925781 to 0.23925781
- boundary_env: bfloat16 [256, 384, 384], P('blk'), may hold values from -6 to 6
- sector_sizes: int32 [16], replicated, may hold values from 110 to 384, as said below
- mpo_ops: float32 [16, 2, 4, 4], replicated, may hold values from -2 to 2
- mpo_mask: int32 [16, 2], replicated, may hold values 0 or 1
Outputs:
- envs: bfloat16 [4, 256, 384, 384], P('sect', 'blk')
- grads: bfloat16 [4, 6144, 1536], P('sect', 'blk')
Inputs may be any that keep to these rules, and one draw needn't show every extreme that they name: `sector_sizes`: exactly one sector holds 384 states, the others hold (1664) // 15 states or one more, and all sizes sum to 2048.
All inputs are finite; a program needn't handle non-finite values.
Results may differ from a plain program's by a relative error of at most 0.018.
Values may be sent and summed in bfloat16 or wider, within the bound.
A program may use at most 64 MiB of HBM per device.

v0:
```python
import jax
import jax.numpy as jnp
from jax import lax
from jax.experimental import pallas as pl
from jax.experimental.pallas import tpu as pltpu
from jax.sharding import PartitionSpec as P

N = 384
T = 128
H = 112
G8 = 8
BF = jnp.bfloat16
F32 = jnp.float32
MESH = pl.DeviceIdType.MESH
DMA = pltpu.SemaphoreType.DMA


def mm(a, b):
    return jnp.dot(a, b, preferred_element_type=F32)


def mm_t(a, b):
    return lax.dot_general(a, b, (((1,), (1,)), ((), ())), preferred_element_type=F32)


def t_mm(a, b):
    return lax.dot_general(a, b, (((0,), (0,)), ((), ())), preferred_element_type=F32)


def mix(coef, prods, target):
    sources = ((0,), (1, 2), (1, 2), (3,))[target]
    out = []
    for w in range(2):
        total = None
        for p in sources:
            for k in range(2):
                term = coef(w, k, p, target) * prods[w ^ k][p].astype(F32)
                total = term if total is None else total + term
        out.append(total.astype(BF))
    return out


def pull_mixed(coef, pull, base, m1, m3):
    prods = []
    zero = jnp.zeros((T - H, T), BF)
    for w in range(2):
        near = jnp.concatenate([m1[w], zero], axis=0)
        far = jnp.concatenate([m3[w], zero], axis=0)
        prods.append(
            (
                None,
                mm(pull[:, base : base + T], near).astype(BF),
                mm(pull[:, base + T : base + 2 * T], near).astype(BF),
                mm(pull[:, base + 2 * T : base + 3 * T], far).astype(BF),
            )
        )
    return [None] + [mix(coef, prods, target) for target in range(1, 4)]


def combine(big, coef, pull, base, c0, m1, m3, put):
    mixed = pull_mixed(coef, pull, base, m1, m3)
    for w in range(2):
        kept = c0[w].astype(F32)
        total = kept
        for p in range(1, 4):
            total = total + mm_t(mixed[p][w], pull[:, base + (p - 1) * T : base + p * T])
        small = kept[:H, :T] + m1[w].astype(F32) + m3[w].astype(F32)
        put(
            w,
            jnp.where(big, total, jnp.zeros_like(total)).astype(BF),
            jnp.where(big, total[:H, :T], small).astype(BF),
        )
    return mixed


def remote(src, dst, sems, slot, target):
    return pltpu.make_async_remote_copy(
        src_ref=src,
        dst_ref=dst,
        send_sem=sems[0].at[slot],
        recv_sem=sems[1].at[slot],
        device_id=target,
        device_id_type=MESH,
    )


def greet(targets):
    barrier = pltpu.get_barrier_semaphore()
    for target in targets:
        pl.semaphore_signal(barrier, inc=1, device_id=target, device_id_type=MESH)
    return barrier


def write_rows(out, grads):
    for within in range(G8):
        spot = (within % 2) * 4 + within // 2
        out[spot] = grads[48 * within : 48 * within + 48].astype(BF)


def sweep_kernel(
    sizes, ops, mask, rows3, bound, left4, env4, grads3,
    acol, pull, xs, hs, ab, right, c0, m1, m3, got0, got1, got3, at1, at3, near_l, far_l,
    mx0, mxh, parts, part_in, sums, sums_in, totals, home,
    send, recv, csend, crecv, gsend, grecv, own_sem,
):
    rows, left, env_out, grads_out = rows3.at[0], left4.at[0], env4.at[0], grads3.at[0]
    sect = lax.axis_index("sect")
    blk = lax.axis_index("blk")
    within = lax.rem(blk, G8)
    base = blk - within
    sector = blk // G8
    core = lax.rem(within, 2)
    chip = within // 2
    upper = lax.rem(sect + 1, 4)
    lower = lax.rem(sect + 3, 4)
    mate = (sect, base + chip * 2 + 1 - core)
    peers = [(sect, base + lax.rem(chip + d, 4) * 2 + core) for d in (1, 2, 3)]
    origin = within // 3
    back8, back16 = lax.rem(blk + 120, 128), lax.rem(blk + 112, 128)
    fore8, fore16 = lax.rem(blk + 8, 128), lax.rem(blk + 16, 128)
    barrier = greet(
        peers
        + [mate, (upper, blk), (lower, blk)]
        + [(sect, lax.rem(base + 128 - 8 * d + origin, 128)) for d in (1, 2)]
        + [(upper, fore8), (upper, fore16), (lower, back8), (lower, back16)]
        + [(sect, back8), (sect, back16), (sect, fore8), (sect, fore16)]
    )
    goals = [[(sect, lax.rem(base + 8 * d, 128) + 3 * within + j) for j in range(3)] for d in (1, 2)]
    sends_halo = [(3 * within + j) < G8 for j in range(3)]
    for j in range(3):

        @pl.when(sends_halo[j])
        def _(j=j):
            for d in range(2):
                pl.semaphore_signal(barrier, inc=1, device_id=goals[d][j], device_id_type=MESH)

    own = [pltpu.make_async_copy(rows.at[:, pl.ds(0, N)], xs.at[within, :, pl.ds(0, N)], own_sem.at[0])]
    for p in range(1, 4):
        own.append(
            pltpu.make_async_copy(
                rows.at[:, pl.ds(N * p, T)], xs.at[within, :, pl.ds(N + T * (p - 1), T)], own_sem.at[p]
            )
        )
    for copy in own:
        copy.start()

    n_own = sizes[sector]
    n_near = jnp.where(sector >= 1, sizes[jnp.maximum(sector - 1, 0)], 0)
    n_far = jnp.where(sector >= 2, sizes[jnp.maximum(sector - 2, 0)], 0)
    big, near_big, far_big = n_own > H, n_near > H, n_far > H

    def coef(w, k, p, target):
        channel = 2 * within + w
        return ops[channel, k, p, target] * mask[channel, k].astype(F32)

    row = lax.broadcasted_iota(jnp.int32, (N, N), 0)
    col = lax.broadcasted_iota(jnp.int32, (N, N), 1)
    live = jnp.maximum(row, col) < n_own
    for w in range(2):
        right[w] = jnp.where(live, bound[w], jnp.zeros((N, N), BF))
    for copy in own:
        copy.wait()
    extra = jnp.where(within < 2, 6, jnp.where(within == 2, 4, 0))
    pl.semaphore_wait(barrier, 16 + extra)

    sems = (send, recv)

    def halo_copy(d, j):
        width = 2 * N if d == 0 else N
        at = N if d == 0 else 3 * N
        to = 0 if d == 0 else 2 * N
        return pltpu.make_async_remote_copy(
            src_ref=rows.at[pl.ds(16 * j, 16), pl.ds(at, width)],
            dst_ref=hs.at[3 * within + j, :, pl.ds(to, width)],
            send_sem=send.at[3 * d + j],
            recv_sem=recv.at[d],
            device_id=goals[d][j],
            device_id_type=MESH,
        )

    for j in range(3):

        @pl.when(sends_halo[j])
        def _(j=j):
            halo_copy(0, j).start()
            halo_copy(1, j).start()

    x_peer = [remote(xs.at[within], xs.at[within], sems, 7 + d, peers[d]) for d in range(3)]
    for copy in x_peer:
        copy.start()
    x_mate = [remote(xs.at[within], xs.at[within], sems, 10, mate)]
    x_mate[0].start()
    above = remote(xs.at[within, :, pl.ds(N, N)], ab.at[within], sems, 6, (lower, blk))
    above.start()
    csems = (csend, crecv)
    l_near = remote(left.at[:, pl.ds(0, H), :], near_l, csems, 6, (sect, fore8))
    l_far = remote(left.at[:, pl.ds(0, H), :], far_l, csems, 7, (sect, fore16))

    def landed(ref, slot):
        pltpu.make_async_remote_copy(
            src_ref=ref,
            dst_ref=ref,
            send_sem=send.at[slot],
            recv_sem=recv.at[slot],
            device_id=mate,
            device_id_type=MESH,
        ).wait_recv()

    landed(hs.at[within, :, pl.ds(0, 2 * N)], 0)
    landed(hs.at[within, :, pl.ds(2 * N, N)], 1)
    h_peer = [remote(hs.at[within], hs.at[within], sems, 21 + d, peers[d]) for d in range(3)]
    h_mate = [remote(hs.at[within], hs.at[within], sems, 24, mate)]
    for copy in h_peer + h_mate:
        copy.start()
    landed(ab.at[within], 6)
    a_peer = [remote(ab.at[within], ab.at[within], sems, 14 + d, peers[d]) for d in range(3)]
    a_mate = [remote(ab.at[within], ab.at[within], sems, 17, mate)]
    for copy in a_peer + a_mate:
        copy.start()

    def pass_on(buf, first, mine):
        for d in range(3):
            spot = lax.rem(chip + 3 - d, 4) * 2 + core
            landed(buf.at[spot], first + d)
            forward = remote(buf.at[spot], buf.at[spot], sems, first + 4 + d, mate)
            forward.start()
            mine.append(forward)

    pass_on(xs, 7, x_mate)
    pass_on(hs, 21, h_mate)
    for copy in x_mate + h_mate:
        copy.wait()
    for w in range(G8):
        line = lax.broadcasted_iota(jnp.int32, (48, N), 0) + 48 * w
        zero = jnp.zeros((48, N), BF)
        acol[48 * w : 48 * w + 48, :] = jnp.where(line < n_own, xs[w, :, :N], zero)
        pull[48 * w : 48 * w + 48, :N] = jnp.where(line < n_own, xs[w, :, N:], zero)
        halo_line = lax.broadcasted_iota(jnp.int32, (16, N), 0) + 16 * w
        for block in range(3):
            limit = n_near if block < 2 else n_far
            at = N + T * block + 16 * w
            acol[at : at + 16, :] = jnp.where(
                halo_line < limit, hs[w, :, N * block : N * block + N], jnp.zeros((16, N), BF)
            )

    def finish_above():
        pass_on(ab, 14, a_mate)
        for copy in a_mate:
            copy.wait()
        for w in range(G8):
            line = lax.broadcasted_iota(jnp.int32, (48, N), 0) + 48 * w
            pull[48 * w : 48 * w + 48, N:] = jnp.where(line < n_own, ab[w], jnp.zeros((48, N), BF))

    @pl.when(sect < 2)
    def _():
        l_near.start()
        l_far.start()

    down0 = [remote(c0.at[w], got0.at[w], csems, 2 + w, (lower, blk)) for w in range(2)]
    down1 = remote(m1, got1, csems, 0, (lower, back8))
    down3 = remote(m3, got3, csems, 1, (lower, back16))
    last1 = remote(m1, at1, csems, 4, (sect, back8))
    last3 = remote(m3, at3, csems, 5, (sect, back16))
    back0 = remote(right, env_out, csems, 8, (upper, blk))
    up1 = remote(got1, at1, csems, 9, (upper, blk))
    up3 = remote(got3, at3, csems, 10, (upper, blk))

    def put_right(w, whole, tile):
        right[w] = whole
        right[w, :H, :T] = tile

    def put_env(w, whole, tile):
        env_out[w] = whole
        env_out[w, :H, :T] = tile

    finish_above()

    @pl.when(sect < 3)
    def _():
        down1.wait_recv()
        down3.wait_recv()
        down0[0].wait_recv()
        down0[1].wait_recv()
        combine(big, coef, pull, N, got0, got1, got3, put_right)

    prods = []
    for w in range(2):
        own_p = mm(acol[:N, :], right[w]).astype(BF)
        halo_p = mm(acol[N : 2 * N, :], right[w]).astype(BF)
        prods.append((own_p, halo_p[:T], halo_p[T : 2 * T], halo_p[2 * T :]))
    for p in range(1, 4):
        blend = mix(coef, prods, p)
        for w in range(2):
            mxh[w, p - 1] = blend[w]
    for w in range(2):
        tile = right[w, :H, :T]
        near = mm_t(mxh[w, 0], acol[N : N + T, :]) + mm_t(mxh[w, 1], acol[N + T : N + 2 * T, :])
        far = mm_t(mxh[w, 2], acol[N + 2 * T : 2 * N, :])
        m1[w] = jnp.where(near_big, tile, near[:H].astype(BF))
        m3[w] = jnp.where(far_big, tile, far[:H].astype(BF))

    @pl.when(sect > 0)
    def _():
        down3.start()
        down1.start()

    @pl.when(sect == 0)
    def _():
        last3.start()
        last1.start()

    blend = mix(coef, prods, 0)
    for w in range(2):
        mx0[w] = blend[w]
        c0[w] = mm_t(blend[w], acol[:N, :]).astype(BF)

        @pl.when(sect > 0)
        def _(w=w):
            down0[w].start()

    @pl.when(sect < 3)
    def _():
        back0.start()
        up1.start()
        up3.start()

    @pl.when(sect >= 2)
    def _():
        l_near.start()
        l_far.start()

    gsems = (gsend, grecv)
    core_copy = [
        remote(parts.at[k, pl.ds((1 - core) * 4, 4)], part_in.at[k], gsems, k, mate) for k in range(5)
    ]
    peer_copy = [
        [
            remote(sums.at[k, lax.rem(chip + d + 1, 4)], sums_in.at[k, d], gsems, 5 + 3 * k + d, peers[d])
            for d in range(3)
        ]
        for k in range(5)
    ]
    home_copy = [
        remote(totals.at[k], home.at[k], gsems, 20 + k, (sect, back16 if k == 0 else back8))
        for k in range(3)
    ]

    def add_core(k):
        core_copy[k].wait_recv()
        mine = parts[k, pl.ds(core * 4, 4)]
        sums[k] = (mine.astype(F32) + part_in[k].astype(F32)).astype(BF)
        for copy in peer_copy[k]:
            copy.start()

    def add_line(k):
        for copy in peer_copy[k]:
            copy.wait_recv()
        total = sums[k, chip].astype(F32)
        for d in range(3):
            total = total + sums_in[k, d].astype(F32)
        totals[k] = total.astype(BF)

    write_rows(parts.at[3], t_mm(left[0], mx0[0]) + t_mm(left[1], mx0[1]))
    core_copy[3].start()
    l_far.wait_recv()
    write_rows(parts.at[0], t_mm(far_l[0], mxh[0, 2, :H]) + t_mm(far_l[1], mxh[1, 2, :H]))
    core_copy[0].start()
    l_near.wait_recv()
    for p in (1, 2):
        write_rows(parts.at[p], t_mm(near_l[0], mxh[0, p - 1, :H]) + t_mm(near_l[1], mxh[1, p - 1, :H]))
        core_copy[p].start()
    for k in (0, 1, 2, 3):
        add_core(k)

    @pl.when(sect == 0)
    def _():
        last1.wait_recv()
        last3.wait_recv()
        combine(big, coef, pull, 0, c0, at1, at3, put_env)

    @pl.when(sect > 0)
    def _():
        up1.wait_recv()
        up3.wait_recv()

    mixed = pull_mixed(coef, pull, 0, at1, at3)
    narrow = [t_mm(left[0], mixed[p][0]) + t_mm(left[1], mixed[p][1]) for p in range(1, 4)]
    write_rows(parts.at[4], jnp.concatenate(narrow, axis=1))
    core_copy[4].start()
    for k in range(3):
        add_line(k)
        home_copy[k].start()
    add_core(4)
    add_line(3)
    add_line(4)
    grads_out[:, :N] = totals[3]
    zero = jnp.zeros((48, N - T), BF)
    for p in range(1, 4):
        k = p % 3
        home_copy[k].wait_recv()
        thin = jnp.concatenate([totals[4, :, T * (p - 1) : T * p], zero], axis=1)
        grads_out[:, N * p : N * p + N] = jnp.where(big, thin, home[k])

    for copy in x_peer + h_peer + a_peer + [above, l_near, l_far] + core_copy + home_copy:
        copy.wait_send()
    for k in range(5):
        for copy in peer_copy[k]:
            copy.wait_send()
    for j in range(3):

        @pl.when(sends_halo[j])
        def _(j=j):
            halo_copy(0, j).wait_send()
            halo_copy(1, j).wait_send()

    @pl.when(sect == 0)
    def _():
        last1.wait_send()
        last3.wait_send()

    @pl.when(sect > 0)
    def _():
        down1.wait_send()
        down3.wait_send()
        down0[0].wait_send()
        down0[1].wait_send()
        back0.wait_recv()

    @pl.when(sect < 3)
    def _():
        back0.wait_send()
        up1.wait_send()
        up3.wait_send()


SMEM = pl.BlockSpec(memory_space=pltpu.SMEM)
VMEM = pl.BlockSpec(memory_space=pltpu.VMEM)


def local(site_tensor, left_env, boundary_env, sector_sizes, mpo_ops, mpo_mask):
    def buf(*shape):
        return pltpu.VMEM(shape, BF)

    return pl.pallas_call(
        sweep_kernel,
        out_shape=(
            jax.ShapeDtypeStruct((1, 2, N, N), BF),
            jax.ShapeDtypeStruct((1, 48, 4 * N), BF),
        ),
        in_specs=[SMEM] * 3 + [VMEM] * 3,
        out_specs=(VMEM, VMEM),
        scratch_shapes=[
            buf(2 * N, N),
            buf(N, 2 * N),
            buf(G8, 48, 2 * N),
            buf(G8, 16, 3 * N),
            buf(G8, 48, N),
            buf(2, N, N),
            buf(2, N, N),
            buf(2, H, T),
            buf(2, H, T),
            buf(2, N, N),
            buf(2, H, T),
            buf(2, H, T),
            buf(2, H, T),
            buf(2, H, T),
            buf(2, H, N),
            buf(2, H, N),
            buf(2, N, N),
            buf(2, 3, T, N),
            buf(5, G8, 48, N),
            buf(5, 4, 48, N),
            buf(5, 4, 48, N),
            buf(5, 3, 48, N),
            buf(5, 48, N),
            buf(3, 48, N),
            DMA((28,)),
            DMA((28,)),
            DMA((11,)),
            DMA((11,)),
            DMA((23,)),
            DMA((23,)),
            DMA((4,)),
        ],
        compiler_params=pltpu.CompilerParams(
            collective_id=0, has_side_effects=True, vmem_limit_bytes=48 * 1024 * 1024
        ),
        name="sweep",
    )(sector_sizes, mpo_ops, mpo_mask, site_tensor, boundary_env, left_env)


def solution(mesh):
    return jax.shard_map(
        local,
        mesh=mesh,
        in_specs=(
            P("sect", "blk", None),
            P("sect", "blk", None, None),
            P("blk", None, None),
            P(),
            P(),
            P(),
        ),
        out_specs=(P("sect", "blk", None, None), P("sect", "blk", None)),
        check_vma=False,
    )
```

profile of v0, /device:TPU:1, one launch (start us, length us, event | category | flops | bytes accessed | tf_op | source)
XLA Modules:
  0.0 144.8 jit_solution(5239795096673848990)
XLA Ops:
  0.6 0.8 copy.9.mask
  1.4 0.0 copy-start.3
  1.4 0.9 copy.8.ops
  2.2 0.0 copy-done.3
  2.2 0.0 copy-start
  2.3 1.1 copy-done
  3.3 0.0 copy-start.1
  3.3 1.1 copy-done.1
  4.4 0.0 copy-start.2
  4.4 0.9 copy-done.2
  5.3 138.0 %sweep.1 = (bf16[1,2,384,384]{3,2,1,0:T(8,128)(2,1)S(1)}, bf16[1,48,1536]{2,1,0:T(8,128)(2,1)S(1)}) custom-call(s32[16]{0:T(128)S(1)} %copy-done.3, f32[16,2,4,4]{3,2,1,0:T(4,128)S(1)} %copy.8.ops, s32[16,2]{1,0:T(8,128)S(1)} %copy.9.mask, bf16[1,48,1536]{2,1,0:T(8,128)(2,1)S(1)} %copy-done.2, bf16[2,384,384]{2,1,0:T(8,128)(2,1)S(1)} %copy-done, ...), custom_call_target="tpu_custom_call" | custom-call | tf_op jit(solution)/shard_map/sweep/pallas_call | solution.py:444
  143.3 0.8 copy.12
  144.2 0.7 copy.13
Async XLA Ops:
  1.4 0.9 copy-start.3
  2.2 1.1 copy-start
  3.3 1.1 copy-start.1
  4.4 0.9 copy-start.2
where the time goes:
time: 145 us
  Pallas kernels  138 us (95%)
  local copies, waits for them, and re-layouts  6.13 us (4%)
    pallas_call x1, Pallas kernels, local(): pl.pallas_call(sweep_kernel, out_shape=(jax.ShapeDtypeStruct((1, 2, N, N)...  138 us
    unnamed x12, local copies, waits for them, and re-layouts  6.13 us

commit v1 on v0

--- a/solution.py
+++ b/solution.py
@@ -40,37 +40,48 @@
     return out
 
 
-def pull_mixed(coef, pull, base, m1, m3):
+def widen(tile):
+    return jnp.concatenate([tile, jnp.zeros((T - H, T), BF)], axis=0)
+
+
+def pull_near(coef, pull, base, m1):
     prods = []
-    zero = jnp.zeros((T - H, T), BF)
     for w in range(2):
-        near = jnp.concatenate([m1[w], zero], axis=0)
-        far = jnp.concatenate([m3[w], zero], axis=0)
+        near = widen(m1[w])
         prods.append(
             (
                 None,
                 mm(pull[:, base : base + T], near).astype(BF),
                 mm(pull[:, base + T : base + 2 * T], near).astype(BF),
-                mm(pull[:, base + 2 * T : base + 3 * T], far).astype(BF),
             )
         )
-    return [None] + [mix(coef, prods, target) for target in range(1, 4)]
-
-
-def combine(big, coef, pull, base, c0, m1, m3, put):
-    mixed = pull_mixed(coef, pull, base, m1, m3)
-    for w in range(2):
-        kept = c0[w].astype(F32)
-        total = kept
-        for p in range(1, 4):
-            total = total + mm_t(mixed[p][w], pull[:, base + (p - 1) * T : base + p * T])
-        small = kept[:H, :T] + m1[w].astype(F32) + m3[w].astype(F32)
-        put(
-            w,
-            jnp.where(big, total, jnp.zeros_like(total)).astype(BF),
-            jnp.where(big, total[:H, :T], small).astype(BF),
-        )
-    return mixed
+    return [mix(coef, prods, 1), mix(coef, prods, 2)]
+
+
+def pull_far(coef, pull, base, m3):
+    prods = [
+        (None, None, None, mm(pull[:, base + 2 * T : base + 3 * T], widen(m3[w])).astype(BF))
+        for w in range(2)
+    ]
+    return mix(coef, prods, 3)
+
+
+def near_terms(mixed, pull, base, w):
+    return mm_t(mixed[0][w], pull[:, base : base + T]) + mm_t(
+        mixed[1][w], pull[:, base + T : base + 2 * T]
+    )
+
+
+def far_term(mixed, pull, base, w):
+    return mm_t(mixed[w], pull[:, base + 2 * T : base + 3 * T])
+
+
+def settle(big, out, w, c0, m1, m3, near, far):
+    kept = c0[w].astype(F32)
+    total = kept + near + far
+    small = kept[:H, :T] + m1[w].astype(F32) + m3[w].astype(F32)
+    out[w] = jnp.where(big, total, jnp.zeros_like(total)).astype(BF)
+    out[w, :H, :T] = jnp.where(big, total[:H, :T], small).astype(BF)
 
 
 def remote(src, dst, sems, slot, target):
@@ -98,12 +109,12 @@
 
 
 def sweep_kernel(
-    sizes, ops, mask, rows3, bound, left4, env4, grads3,
-    acol, pull, xs, hs, ab, right, c0, m1, m3, got0, got1, got3, at1, at3, near_l, far_l,
-    mx0, mxh, parts, part_in, sums, sums_in, totals, home,
+    sizes, ops, mask, rows3, bound_hbm, left4, env4, grads3,
+    bound, left, near_acc, acol, pull, xs, hs, ab, right, c0, m1, m3, got0, got1, got3, at1, at3, near_l, far_l,
+    mx0, mxh, mx_pull, parts, part_in, sums, sums_in, totals, home,
     send, recv, csend, crecv, gsend, grecv, own_sem,
 ):
-    rows, left, env_out, grads_out = rows3.at[0], left4.at[0], env4.at[0], grads3.at[0]
+    rows, left_hbm, env_out, grads_out = rows3.at[0], left4.at[0], env4.at[0], grads3.at[0]
     sect = lax.axis_index("sect")
     blk = lax.axis_index("blk")
     within = lax.rem(blk, G8)
@@ -143,6 +154,10 @@
         )
     for copy in own:
         copy.start()
+    bound_in = pltpu.make_async_copy(bound_hbm, bound, own_sem.at[4])
+    left_in = pltpu.make_async_copy(left_hbm, left, own_sem.at[5])
+    bound_in.start()
+    left_in.start()
 
     n_own = sizes[sector]
     n_near = jnp.where(sector >= 1, sizes[jnp.maximum(sector - 1, 0)], 0)
@@ -151,8 +166,9 @@
 
     def coef(w, k, p, target):
         channel = 2 * within + w
-        return ops[channel, k, p, target] * mask[channel, k].astype(F32)
-
+        return ops[k, p, target, channel] * mask[k, channel].astype(F32)
+
+    bound_in.wait()
     row = lax.broadcasted_iota(jnp.int32, (N, N), 0)
     col = lax.broadcasted_iota(jnp.int32, (N, N), 1)
     live = jnp.maximum(row, col) < n_own
@@ -193,8 +209,8 @@
     above = remote(xs.at[within, :, pl.ds(N, N)], ab.at[within], sems, 6, (lower, blk))
     above.start()
     csems = (csend, crecv)
-    l_near = remote(left.at[:, pl.ds(0, H), :], near_l, csems, 6, (sect, fore8))
-    l_far = remote(left.at[:, pl.ds(0, H), :], far_l, csems, 7, (sect, fore16))
+    l_near = remote(left_hbm.at[:, pl.ds(0, H), :], near_l, csems, 6, (sect, fore8))
+    l_far = remote(left_hbm.at[:, pl.ds(0, H), :], far_l, csems, 7, (sect, fore16))
 
     def landed(ref, slot):
         pltpu.make_async_remote_copy(
@@ -226,36 +242,6 @@
             forward.start()
             mine.append(forward)
 
-    pass_on(xs, 7, x_mate)
-    pass_on(hs, 21, h_mate)
-    for copy in x_mate + h_mate:
-        copy.wait()
-    for w in range(G8):
-        line = lax.broadcasted_iota(jnp.int32, (48, N), 0) + 48 * w
-        zero = jnp.zeros((48, N), BF)
-        acol[48 * w : 48 * w + 48, :] = jnp.where(line < n_own, xs[w, :, :N], zero)
-        pull[48 * w : 48 * w + 48, :N] = jnp.where(line < n_own, xs[w, :, N:], zero)
-        halo_line = lax.broadcasted_iota(jnp.int32, (16, N), 0) + 16 * w
-        for block in range(3):
-            limit = n_near if block < 2 else n_far
-            at = N + T * block + 16 * w
-            acol[at : at + 16, :] = jnp.where(
-                halo_line < limit, hs[w, :, N * block : N * block + N], jnp.zeros((16, N), BF)
-            )
-
-    def finish_above():
-        pass_on(ab, 14, a_mate)
-        for copy in a_mate:
-            copy.wait()
-        for w in range(G8):
-            line = lax.broadcasted_iota(jnp.int32, (48, N), 0) + 48 * w
-            pull[48 * w : 48 * w + 48, N:] = jnp.where(line < n_own, ab[w], jnp.zeros((48, N), BF))
-
-    @pl.when(sect < 2)
-    def _():
-        l_near.start()
-        l_far.start()
-
     down0 = [remote(c0.at[w], got0.at[w], csems, 2 + w, (lower, blk)) for w in range(2)]
     down1 = remote(m1, got1, csems, 0, (lower, back8))
     down3 = remote(m3, got3, csems, 1, (lower, back16))
@@ -265,69 +251,125 @@
     up1 = remote(got1, at1, csems, 9, (upper, blk))
     up3 = remote(got3, at3, csems, 10, (upper, blk))
 
-    def put_right(w, whole, tile):
-        right[w] = whole
-        right[w, :H, :T] = tile
-
-    def put_env(w, whole, tile):
-        env_out[w] = whole
-        env_out[w, :H, :T] = tile
-
-    finish_above()
+    def own_terms():
+        prods = [(mm(acol[:N, :], right[w]).astype(BF),) for w in range(2)]
+        blend = mix(coef, prods, 0)
+        for w in range(2):
+            mx0[w] = blend[w]
+            c0[w] = mm_t(blend[w], acol[:N, :]).astype(BF)
+
+            @pl.when(sect > 0)
+            def _(w=w):
+                down0[w].start()
+
+    def finish_above():
+        pass_on(ab, 14, [])
+        for d in range(3):
+            remote(ab.at[within], ab.at[within], sems, 18 + d, mate).wait()
+        a_mate[0].wait()
+        for w in range(G8):
+            line = lax.broadcasted_iota(jnp.int32, (48, N), 0) + 48 * w
+            pull[48 * w : 48 * w + 48, N:] = jnp.where(line < n_own, ab[w], jnp.zeros((48, N), BF))
+
+    pass_on(xs, 7, x_mate)
+    for copy in x_mate:
+        copy.wait()
+    for w in range(G8):
+        line = lax.broadcasted_iota(jnp.int32, (48, N), 0) + 48 * w
+        acol[48 * w : 48 * w + 48, :] = jnp.where(line < n_own, xs[w, :, :N], jnp.zeros((48, N), BF))
+
+    @pl.when(sect == 3)
+    def _():
+        own_terms()
+
+    pass_on(hs, 21, h_mate)
+    for copy in h_mate:
+        copy.wait()
+    for w in range(G8):
+        halo_line = lax.broadcasted_iota(jnp.int32, (16, N), 0) + 16 * w
+        for block in range(3):
+            limit = n_near if block < 2 else n_far
+            at = N + T * block + 16 * w
+            acol[at : at + 16, :] = jnp.where(
+                halo_line < limit, hs[w, :, N * block : N * block + N], jnp.zeros((16, N), BF)
+            )
+
+    @pl.when(sect < 2)
+    def _():
+        l_near.start()
+        l_far.start()
 
     @pl.when(sect < 3)
     def _():
+        finish_above()
         down1.wait_recv()
+        mixed = pull_near(coef, pull, N, got1)
+        for w in range(2):
+            near_acc[w] = near_terms(mixed, pull, N, w)
         down3.wait_recv()
-        down0[0].wait_recv()
-        down0[1].wait_recv()
-        combine(big, coef, pull, N, got0, got1, got3, put_right)
-
-    prods = []
+        mixed = pull_far(coef, pull, N, got3)
+        for w in range(2):
+            down0[w].wait_recv()
+            settle(big, right, w, got0, got1, got3, near_acc[w], far_term(mixed, pull, N, w))
+
+    far_p = [
+        (None, None, None, mm(acol[N + 2 * T : 2 * N, :], right[w]).astype(BF)) for w in range(2)
+    ]
+    blend = mix(coef, far_p, 3)
     for w in range(2):
-        own_p = mm(acol[:N, :], right[w]).astype(BF)
-        halo_p = mm(acol[N : 2 * N, :], right[w]).astype(BF)
-        prods.append((own_p, halo_p[:T], halo_p[T : 2 * T], halo_p[2 * T :]))
-    for p in range(1, 4):
-        blend = mix(coef, prods, p)
-        for w in range(2):
-            mxh[w, p - 1] = blend[w]
+        mxh[w, 2] = blend[w]
+        far = mm_t(blend[w], acol[N + 2 * T : 2 * N, :])
+        m3[w] = jnp.where(far_big, right[w, :H, :T], far[:H].astype(BF))
+
+    @pl.when(sect > 0)
+    def _():
+        down3.start()
+
+    @pl.when(sect == 0)
+    def _():
+        last3.start()
+
+    @pl.when(sect < 3)
+    def _():
+        own_terms()
+
+    near_p = []
     for w in range(2):
-        tile = right[w, :H, :T]
-        near = mm_t(mxh[w, 0], acol[N : N + T, :]) + mm_t(mxh[w, 1], acol[N + T : N + 2 * T, :])
-        far = mm_t(mxh[w, 2], acol[N + 2 * T : 2 * N, :])
-        m1[w] = jnp.where(near_big, tile, near[:H].astype(BF))
-        m3[w] = jnp.where(far_big, tile, far[:H].astype(BF))
+        both = mm(acol[N : N + 2 * T, :], right[w]).astype(BF)
+        near_p.append((None, both[:T], both[T:]))
+    blend = [mix(coef, near_p, p) for p in (1, 2)]
+    for w in range(2):
+        mxh[w, 0] = blend[0][w]
+        mxh[w, 1] = blend[1][w]
+        near = mm_t(blend[0][w], acol[N : N + T, :]) + mm_t(blend[1][w], acol[N + T : N + 2 * T, :])
+        m1[w] = jnp.where(near_big, right[w, :H, :T], near[:H].astype(BF))
 
     @pl.when(sect > 0)
     def _():
-        down3.start()
         down1.start()
 
     @pl.when(sect == 0)
     def _():
-        last3.start()
         last1.start()
 
-    blend = mix(coef, prods, 0)
-    for w in range(2):
-        mx0[w] = blend[w]
-        c0[w] = mm_t(blend[w], acol[:N, :]).astype(BF)
-
-        @pl.when(sect > 0)
-        def _(w=w):
-            down0[w].start()
-
     @pl.when(sect < 3)
     def _():
-        back0.start()
         up1.start()
         up3.start()
+        back0.start()
 
     @pl.when(sect >= 2)
     def _():
         l_near.start()
         l_far.start()
+
+    @pl.when(sect == 3)
+    def _():
+        finish_above()
+
+    for w in range(G8):
+        line = lax.broadcasted_iota(jnp.int32, (48, N), 0) + 48 * w
+        pull[48 * w : 48 * w + 48, :N] = jnp.where(line < n_own, xs[w, :, N:], jnp.zeros((48, N), BF))
 
     gsems = (gsend, grecv)
     core_copy = [
@@ -360,8 +402,7 @@
             total = total + sums_in[k, d].astype(F32)
         totals[k] = total.astype(BF)
 
-    write_rows(parts.at[3], t_mm(left[0], mx0[0]) + t_mm(left[1], mx0[1]))
-    core_copy[3].start()
+    left_in.wait()
     l_far.wait_recv()
     write_rows(parts.at[0], t_mm(far_l[0], mxh[0, 2, :H]) + t_mm(far_l[1], mxh[1, 2, :H]))
     core_copy[0].start()
@@ -369,29 +410,43 @@
     for p in (1, 2):
         write_rows(parts.at[p], t_mm(near_l[0], mxh[0, p - 1, :H]) + t_mm(near_l[1], mxh[1, p - 1, :H]))
         core_copy[p].start()
-    for k in (0, 1, 2, 3):
+    add_core(0)
+    write_rows(parts.at[3], t_mm(left[0], mx0[0]) + t_mm(left[1], mx0[1]))
+    core_copy[3].start()
+    for k in (1, 2, 3):
         add_core(k)
-
-    @pl.when(sect == 0)
-    def _():
-        last1.wait_recv()
-        last3.wait_recv()
-        combine(big, coef, pull, 0, c0, at1, at3, put_env)
-
-    @pl.when(sect > 0)
-    def _():
-        up1.wait_recv()
-        up3.wait_recv()
-
-    mixed = pull_mixed(coef, pull, 0, at1, at3)
-    narrow = [t_mm(left[0], mixed[p][0]) + t_mm(left[1], mixed[p][1]) for p in range(1, 4)]
-    write_rows(parts.at[4], jnp.concatenate(narrow, axis=1))
-    core_copy[4].start()
     for k in range(3):
         add_line(k)
         home_copy[k].start()
+
+    @pl.when(sect == 0)
+    def _():
+        last1.wait_recv()
+        last3.wait_recv()
+
+    @pl.when(sect > 0)
+    def _():
+        up1.wait_recv()
+        up3.wait_recv()
+
+    mixed = pull_near(coef, pull, 0, at1)
+    mixed.append(pull_far(coef, pull, 0, at3))
+    narrow = [t_mm(left[0], mixed[p][0]) + t_mm(left[1], mixed[p][1]) for p in range(3)]
+    write_rows(parts.at[4], jnp.concatenate(narrow, axis=1))
+    core_copy[4].start()
+    add_line(3)
+    for p in range(3):
+        for w in range(2):
+            mx_pull[w, p] = mixed[p][w]
     add_core(4)
-    add_line(3)
+
+    @pl.when(sect == 0)
+    def _():
+        for w in range(2):
+            near = mm_t(mx_pull[w, 0], pull[:, :T]) + mm_t(mx_pull[w, 1], pull[:, T : 2 * T])
+            far = mm_t(mx_pull[w, 2], pull[:, 2 * T : 3 * T])
+            settle(big, env_out, w, c0, at1, at3, near, far)
+
     add_line(4)
     grads_out[:, :N] = totals[3]
     zero = jnp.zeros((48, N - T), BF)
@@ -435,6 +490,7 @@
 
 SMEM = pl.BlockSpec(memory_space=pltpu.SMEM)
 VMEM = pl.BlockSpec(memory_space=pltpu.VMEM)
+HBM = pl.BlockSpec(memory_space=pltpu.HBM)
 
 
 def local(site_tensor, left_env, boundary_env, sector_sizes, mpo_ops, mpo_mask):
@@ -447,9 +503,12 @@
             jax.ShapeDtypeStruct((1, 2, N, N), BF),
             jax.ShapeDtypeStruct((1, 48, 4 * N), BF),
         ),
-        in_specs=[SMEM] * 3 + [VMEM] * 3,
+        in_specs=[SMEM] * 3 + [HBM] * 3,
         out_specs=(VMEM, VMEM),
         scratch_shapes=[
+            buf(2, N, N),
+            buf(2, N, N),
+            pltpu.VMEM((2, N, N), F32),
             buf(2 * N, N),
             buf(N, 2 * N),
             buf(G8, 48, 2 * N),
@@ -468,6 +527,7 @@
             buf(2, H, N),
             buf(2, N, N),
             buf(2, 3, T, N),
+            buf(2, 3, N, T),
             buf(5, G8, 48, N),
             buf(5, 4, 48, N),
             buf(5, 4, 48, N),
@@ -480,13 +540,20 @@
             DMA((11,)),
             DMA((23,)),
             DMA((23,)),
-            DMA((4,)),
+            DMA((6,)),
         ],
         compiler_params=pltpu.CompilerParams(
-            collective_id=0, has_side_effects=True, vmem_limit_bytes=48 * 1024 * 1024
+            collective_id=0, has_side_effects=True, vmem_limit_bytes=64_000_000
         ),
         name="sweep",
-    )(sector_sizes, mpo_ops, mpo_mask, site_tensor, boundary_env, left_env)
+    )(
+        sector_sizes,
+        jnp.transpose(mpo_ops, (1, 2, 3, 0)),
+        jnp.transpose(mpo_mask, (1, 0)),
+        site_tensor,
+        boundary_env,
+        left_env,
+    )
 
 
 def solution(mesh):

time: 145 us -> 137 us (0.945)
  Pallas kernels: 138 us -> 132 us
  local copies, waits for them, and re-layouts: 6.13 us -> 2.64 us
    pallas_call x1, Pallas kernels: 138 us -> 132 us  [local(): pl.pallas_call(sweep_kernel, out_shape=(jax.ShapeDtypeStruct((1, 2, N, N)...]
    unnamed x12 -> x4, local copies, waits for them, and re-layouts: 6.13 us -> 2.64 us
where the time goes in v1:
time: 137 us; the launch traced here: 136 us
  Pallas kernels  132 us (96%)
  local copies, waits for them, and re-layouts  2.64 us (2%)
    pallas_call x1, Pallas kernels, local(): pl.pallas_call(sweep_kernel, out_shape=(jax.ShapeDtypeStruct((1, 2, N, N)...  132 us

profile of v1, /device:TPU:1, one launch (start us, length us, event | category | flops | bytes accessed | tf_op | source)
XLA Modules:
  0.0 135.7 jit_solution(14293725185078551594)
XLA Ops:
  0.6 132.4 %sweep.1 = (bf16[1,2,384,384]{3,2,1,0:T(8,128)(2,1)}, bf16[1,48,1536]{2,1,0:T(8,128)(2,1)}) custom-call(s32[16]{0:T(128)} %sizes.1, f32[2,4,4,16]{3,2,1,0:T(4,128)} %bitcast.2, s32[2,16]{1,0:T(2,128)} %bitcast.3, bf16[1,48,1536]{2,1,0:T(8,128)(2,1)} %rows3.1, bf16[2,384,384]{2,1,0:T(8,128)(2,1)} %bound_hbm.1, bf16[1,2,384,384]{3,2,1,0:T(8,128)(2,1)} %left4.1), custom_call_target="tpu_custom_call" | custom-call | tf_op jit(solution)/shard_map/sweep/pallas_call | solution.py:500
  133.0 0.0 copy-start
  133.0 2.0 %copy.10 = bf16[1,2,384,384]{3,2,1,0:T(8,128)(2,1)} copy(bf16[1,2,384,384]{3,2,1,0:T(8,128)(2,1)} %get-tuple-element.4) | data formatting | bytes 1179648
  135.0 0.0 copy-done
  135.0 0.7 copy.11
Async XLA Ops:
  133.0 2.0 %copy-start = (bf16[1,48,1536]{2,1,0:T(8,128)(2,1)S(1)}, bf16[1,48,1536]{2,1,0:T(8,128)(2,1)}, u32[]{:S(2)}) copy-start(bf16[1,48,1536]{2,1,0:T(8,128)(2,1)} %get-tuple-element.5) | copy-start | bytes 442372

commit v2 on v1

--- a/solution.py
+++ b/solution.py
@@ -104,14 +104,15 @@
 
 def write_rows(out, grads):
     for within in range(G8):
-        spot = (within % 2) * 4 + within // 2
+        chip = within // 2
+        spot = (within % 2) * 4 + (chip % 2) * 2 + chip // 2
         out[spot] = grads[48 * within : 48 * within + 48].astype(BF)
 
 
 def sweep_kernel(
     sizes, ops, mask, rows3, bound_hbm, left4, env4, grads3,
     bound, left, near_acc, acol, pull, xs, hs, ab, right, c0, m1, m3, got0, got1, got3, at1, at3, near_l, far_l,
-    mx0, mxh, mx_pull, parts, part_in, sums, sums_in, totals, home,
+    mx0, mxh, mx_pull, parts, part_in, sums, sums_in, mids, mids_in, totals, home,
     send, recv, csend, crecv, gsend, grecv, own_sem,
 ):
     rows, left_hbm, env_out, grads_out = rows3.at[0], left4.at[0], env4.at[0], grads3.at[0]
@@ -210,7 +211,7 @@
     above.start()
     csems = (csend, crecv)
     l_near = remote(left_hbm.at[:, pl.ds(0, H), :], near_l, csems, 6, (sect, fore8))
-    l_far = remote(left_hbm.at[:, pl.ds(0, H), :], far_l, csems, 7, (sect, fore16))
+    l_far = remote(near_l, far_l, csems, 7, (sect, fore8))
 
     def landed(ref, slot):
         pltpu.make_async_remote_copy(
@@ -297,11 +298,16 @@
     @pl.when(sect < 2)
     def _():
         l_near.start()
+        finish_above()
+        l_near.wait_recv()
         l_far.start()
 
+    @pl.when(sect == 2)
+    def _():
+        finish_above()
+
     @pl.when(sect < 3)
     def _():
-        finish_above()
         down1.wait_recv()
         mixed = pull_near(coef, pull, N, got1)
         for w in range(2):
@@ -361,7 +367,6 @@
     @pl.when(sect >= 2)
     def _():
         l_near.start()
-        l_far.start()
 
     @pl.when(sect == 3)
     def _():
@@ -375,15 +380,18 @@
     core_copy = [
         remote(parts.at[k, pl.ds((1 - core) * 4, 4)], part_in.at[k], gsems, k, mate) for k in range(5)
     ]
-    peer_copy = [
-        [
-            remote(sums.at[k, lax.rem(chip + d + 1, 4)], sums_in.at[k, d], gsems, 5 + 3 * k + d, peers[d])
-            for d in range(3)
-        ]
+    odd, half = lax.rem(chip, 2), chip // 2
+    side = (sect, base + (chip + 1 - 2 * odd) * 2 + core)
+    across = (sect, base + lax.rem(chip + 2, 4) * 2 + core)
+    side_copy = [
+        remote(sums.at[k, pl.ds((1 - odd) * 2, 2)], sums_in.at[k], gsems, 5 + k, side)
         for k in range(5)
     ]
+    across_copy = [
+        remote(mids.at[k, 1 - half], mids_in.at[k], gsems, 10 + k, across) for k in range(5)
+    ]
     home_copy = [
-        remote(totals.at[k], home.at[k], gsems, 20 + k, (sect, back16 if k == 0 else back8))
+        remote(totals.at[k], home.at[k], gsems, 15 + k, (sect, back16 if k == 0 else back8))
         for k in range(3)
     ]
 
@@ -391,33 +399,44 @@
         core_copy[k].wait_recv()
         mine = parts[k, pl.ds(core * 4, 4)]
         sums[k] = (mine.astype(F32) + part_in[k].astype(F32)).astype(BF)
-        for copy in peer_copy[k]:
-            copy.start()
-
-    def add_line(k):
-        for copy in peer_copy[k]:
-            copy.wait_recv()
-        total = sums[k, chip].astype(F32)
-        for d in range(3):
-            total = total + sums_in[k, d].astype(F32)
-        totals[k] = total.astype(BF)
+        side_copy[k].start()
+
+    def add_side(k):
+        side_copy[k].wait_recv()
+        mine = sums[k, pl.ds(odd * 2, 2)]
+        mids[k] = (mine.astype(F32) + sums_in[k].astype(F32)).astype(BF)
+        across_copy[k].start()
+
+    def add_across(k):
+        across_copy[k].wait_recv()
+        totals[k] = (mids[k, half].astype(F32) + mids_in[k].astype(F32)).astype(BF)
 
     left_in.wait()
+
+    @pl.when(sect >= 2)
+    def _():
+        l_near.wait_recv()
+        l_far.start()
+
+    for p in (1, 2):
+        write_rows(parts.at[p], t_mm(near_l[0], mxh[0, p - 1, :H]) + t_mm(near_l[1], mxh[1, p - 1, :H]))
+        core_copy[p].start()
     l_far.wait_recv()
     write_rows(parts.at[0], t_mm(far_l[0], mxh[0, 2, :H]) + t_mm(far_l[1], mxh[1, 2, :H]))
     core_copy[0].start()
-    l_near.wait_recv()
-    for p in (1, 2):
-        write_rows(parts.at[p], t_mm(near_l[0], mxh[0, p - 1, :H]) + t_mm(near_l[1], mxh[1, p - 1, :H]))
-        core_copy[p].start()
-    add_core(0)
+    add_core(1)
+    add_core(2)
     write_rows(parts.at[3], t_mm(left[0], mx0[0]) + t_mm(left[1], mx0[1]))
     core_copy[3].start()
-    for k in (1, 2, 3):
-        add_core(k)
-    for k in range(3):
-        add_line(k)
+    add_core(0)
+    add_side(1)
+    add_side(2)
+    add_side(0)
+    add_core(3)
+    for k in (1, 2, 0):
+        add_across(k)
         home_copy[k].start()
+    add_side(3)
 
     @pl.when(sect == 0)
     def _():
@@ -434,11 +453,12 @@
     narrow = [t_mm(left[0], mixed[p][0]) + t_mm(left[1], mixed[p][1]) for p in range(3)]
     write_rows(parts.at[4], jnp.concatenate(narrow, axis=1))
     core_copy[4].start()
-    add_line(3)
+    add_across(3)
     for p in range(3):
         for w in range(2):
             mx_pull[w, p] = mixed[p][w]
     add_core(4)
+    add_side(4)
 
     @pl.when(sect == 0)
     def _():
@@ -447,7 +467,7 @@
             far = mm_t(mx_pull[w, 2], pull[:, 2 * T : 3 * T])
             settle(big, env_out, w, c0, at1, at3, near, far)
 
-    add_line(4)
+    add_across(4)
     grads_out[:, :N] = totals[3]
     zero = jnp.zeros((48, N - T), BF)
     for p in range(1, 4):
@@ -458,9 +478,8 @@
 
     for copy in x_peer + h_peer + a_peer + [above, l_near, l_far] + core_copy + home_copy:
         copy.wait_send()
-    for k in range(5):
-        for copy in peer_copy[k]:
-            copy.wait_send()
+    for copy in side_copy + across_copy:
+        copy.wait_send()
     for j in range(3):
 
         @pl.when(sends_halo[j])
@@ -531,15 +550,17 @@
             buf(5, G8, 48, N),
             buf(5, 4, 48, N),
             buf(5, 4, 48, N),
-            buf(5, 3, 48, N),
+            buf(5, 2, 48, N),
+            buf(5, 2, 48, N),
+            buf(5, 48, N),
             buf(5, 48, N),
             buf(3, 48, N),
             DMA((28,)),
             DMA((28,)),
             DMA((11,)),
             DMA((11,)),
-            DMA((23,)),
-            DMA((23,)),
+            DMA((18,)),
+            DMA((18,)),
             DMA((6,)),
         ],
         compiler_params=pltpu.CompilerParams(

time: 137 us -> 128 us (0.934)
  Pallas kernels: 132 us -> 123 us
    pallas_call x1, Pallas kernels: 132 us -> 123 us  [local(): pl.pallas_call(sweep_kernel, out_shape=(jax.ShapeDtypeStruct((1, 2, N, N)...]
where the time goes in v2:
time: 128 us; the launch traced here: 127 us
  Pallas kernels  123 us (96%)
  local copies, waits for them, and re-layouts  2.64 us (2%)
    pallas_call x1, Pallas kernels, local(): pl.pallas_call(sweep_kernel, out_shape=(jax.ShapeDtypeStruct((1, 2, N, N)...  123 us
    unnamed x4, local copies, waits for them, and re-layouts  2.64 us

profile of v2, /device:TPU:1, one launch (start us, length us, event | category | flops | bytes accessed | tf_op | source)
XLA Modules:
  0.0 126.7 jit_solution(11814537959663700193)
XLA Ops:
  0.6 123.4 %sweep.1 = (bf16[1,2,384,384]{3,2,1,0:T(8,128)(2,1)}, bf16[1,48,1536]{2,1,0:T(8,128)(2,1)}) custom-call(s32[16]{0:T(128)} %sizes.1, f32[2,4,4,16]{3,2,1,0:T(4,128)} %bitcast.2, s32[2,16]{1,0:T(2,128)} %bitcast.3, bf16[1,48,1536]{2,1,0:T(8,128)(2,1)} %rows3.1, bf16[2,384,384]{2,1,0:T(8,128)(2,1)} %bound_hbm.1, bf16[1,2,384,384]{3,2,1,0:T(8,128)(2,1)} %left4.1), custom_call_target="tpu_custom_call" | custom-call | tf_op jit(solution)/shard_map/sweep/pallas_call | solution.py:519
  124.0 0.0 copy-start
  124.0 2.0 %copy.10 = bf16[1,2,384,384]{3,2,1,0:T(8,128)(2,1)} copy(bf16[1,2,384,384]{3,2,1,0:T(8,128)(2,1)} %get-tuple-element.4) | data formatting | bytes 1179648
  126.0 0.0 copy-done
  126.0 0.7 copy.11
Async XLA Ops:
  124.0 2.0 %copy-start = (bf16[1,48,1536]{2,1,0:T(8,128)(2,1)S(1)}, bf16[1,48,1536]{2,1,0:T(8,128)(2,1)}, u32[]{:S(2)}) copy-start(bf16[1,48,1536]{2,1,0:T(8,128)(2,1)} %get-tuple-element.5) | copy-start | bytes 442372

commit v3 on v2

--- a/solution.py
+++ b/solution.py
@@ -111,7 +111,7 @@
 
 def sweep_kernel(
     sizes, ops, mask, rows3, bound_hbm, left4, env4, grads3,
-    bound, left, near_acc, acol, pull, xs, hs, ab, right, c0, m1, m3, got0, got1, got3, at1, at3, near_l, far_l,
+    bound, left, near_acc, acol, pull, xs, hn, hf, ab, right, c0, m1, m3, got0, got1, got3, at1, at3, near_l, far_l,
     mx0, mxh, mx_pull, parts, part_in, sums, sums_in, mids, mids_in, totals, home,
     send, recv, csend, crecv, gsend, grecv, own_sem,
 ):
@@ -185,10 +185,9 @@
     def halo_copy(d, j):
         width = 2 * N if d == 0 else N
         at = N if d == 0 else 3 * N
-        to = 0 if d == 0 else 2 * N
         return pltpu.make_async_remote_copy(
             src_ref=rows.at[pl.ds(16 * j, 16), pl.ds(at, width)],
-            dst_ref=hs.at[3 * within + j, :, pl.ds(to, width)],
+            dst_ref=(hn if d == 0 else hf).at[3 * within + j],
             send_sem=send.at[3 * d + j],
             recv_sem=recv.at[d],
             device_id=goals[d][j],
@@ -199,8 +198,8 @@
 
         @pl.when(sends_halo[j])
         def _(j=j):
+            halo_copy(1, j).start()
             halo_copy(0, j).start()
-            halo_copy(1, j).start()
 
     x_peer = [remote(xs.at[within], xs.at[within], sems, 7 + d, peers[d]) for d in range(3)]
     for copy in x_peer:
@@ -223,10 +222,14 @@
             device_id_type=MESH,
         ).wait_recv()
 
-    landed(hs.at[within, :, pl.ds(0, 2 * N)], 0)
-    landed(hs.at[within, :, pl.ds(2 * N, N)], 1)
-    h_peer = [remote(hs.at[within], hs.at[within], sems, 21 + d, peers[d]) for d in range(3)]
-    h_mate = [remote(hs.at[within], hs.at[within], sems, 24, mate)]
+    landed(hf.at[within], 1)
+    f_peer = [remote(hf.at[within], hf.at[within], sems, 28 + d, peers[d]) for d in range(3)]
+    f_mate = [remote(hf.at[within], hf.at[within], sems, 31, mate)]
+    for copy in f_peer + f_mate:
+        copy.start()
+    landed(hn.at[within], 0)
+    h_peer = [remote(hn.at[within], hn.at[within], sems, 21 + d, peers[d]) for d in range(3)]
+    h_mate = [remote(hn.at[within], hn.at[within], sems, 24, mate)]
     for copy in h_peer + h_mate:
         copy.start()
     landed(ab.at[within], 6)
@@ -283,27 +286,38 @@
     def _():
         own_terms()
 
-    pass_on(hs, 21, h_mate)
-    for copy in h_mate:
+    pass_on(hf, 28, f_mate)
+    for copy in f_mate:
         copy.wait()
     for w in range(G8):
         halo_line = lax.broadcasted_iota(jnp.int32, (16, N), 0) + 16 * w
-        for block in range(3):
-            limit = n_near if block < 2 else n_far
-            at = N + T * block + 16 * w
-            acol[at : at + 16, :] = jnp.where(
-                halo_line < limit, hs[w, :, N * block : N * block + N], jnp.zeros((16, N), BF)
-            )
+        at = N + 2 * T + 16 * w
+        acol[at : at + 16, :] = jnp.where(halo_line < n_far, hf[w], jnp.zeros((16, N), BF))
+
+    def finish_near():
+        pass_on(hn, 21, [])
+        for d in range(3):
+            remote(hn.at[within], hn.at[within], sems, 25 + d, mate).wait()
+        h_mate[0].wait()
+        for w in range(G8):
+            halo_line = lax.broadcasted_iota(jnp.int32, (16, N), 0) + 16 * w
+            for block in range(2):
+                at = N + T * block + 16 * w
+                acol[at : at + 16, :] = jnp.where(
+                    halo_line < n_near, hn[w, :, N * block : N * block + N], jnp.zeros((16, N), BF)
+                )
 
     @pl.when(sect < 2)
     def _():
         l_near.start()
+        finish_near()
         finish_above()
         l_near.wait_recv()
         l_far.start()
 
     @pl.when(sect == 2)
     def _():
+        finish_near()
         finish_above()
 
     @pl.when(sect < 3)
@@ -338,6 +352,10 @@
     @pl.when(sect < 3)
     def _():
         own_terms()
+
+    @pl.when(sect == 3)
+    def _():
+        finish_near()
 
     near_p = []
     for w in range(2):
@@ -418,25 +436,28 @@
         l_near.wait_recv()
         l_far.start()
 
+    l_far.wait_recv()
+    write_rows(parts.at[0], t_mm(far_l[0], mxh[0, 2, :H]) + t_mm(far_l[1], mxh[1, 2, :H]))
+    core_copy[0].start()
     for p in (1, 2):
         write_rows(parts.at[p], t_mm(near_l[0], mxh[0, p - 1, :H]) + t_mm(near_l[1], mxh[1, p - 1, :H]))
         core_copy[p].start()
-    l_far.wait_recv()
-    write_rows(parts.at[0], t_mm(far_l[0], mxh[0, 2, :H]) + t_mm(far_l[1], mxh[1, 2, :H]))
-    core_copy[0].start()
+        if p == 1:
+            add_core(0)
     add_core(1)
-    add_core(2)
     write_rows(parts.at[3], t_mm(left[0], mx0[0]) + t_mm(left[1], mx0[1]))
     core_copy[3].start()
-    add_core(0)
+    add_side(0)
+    add_core(2)
     add_side(1)
+    add_across(0)
+    home_copy[0].start()
+    add_core(3)
     add_side(2)
-    add_side(0)
-    add_core(3)
-    for k in (1, 2, 0):
-        add_across(k)
-        home_copy[k].start()
-    add_side(3)
+    add_across(1)
+    home_copy[1].start()
+    add_across(2)
+    home_copy[2].start()
 
     @pl.when(sect == 0)
     def _():
@@ -453,12 +474,12 @@
     narrow = [t_mm(left[0], mixed[p][0]) + t_mm(left[1], mixed[p][1]) for p in range(3)]
     write_rows(parts.at[4], jnp.concatenate(narrow, axis=1))
     core_copy[4].start()
-    add_across(3)
+    add_side(3)
     for p in range(3):
         for w in range(2):
             mx_pull[w, p] = mixed[p][w]
     add_core(4)
-    add_side(4)
+    add_across(3)
 
     @pl.when(sect == 0)
     def _():
@@ -467,6 +488,7 @@
             far = mm_t(mx_pull[w, 2], pull[:, 2 * T : 3 * T])
             settle(big, env_out, w, c0, at1, at3, near, far)
 
+    add_side(4)
     add_across(4)
     grads_out[:, :N] = totals[3]
     zero = jnp.zeros((48, N - T), BF)
@@ -476,7 +498,7 @@
         thin = jnp.concatenate([totals[4, :, T * (p - 1) : T * p], zero], axis=1)
         grads_out[:, N * p : N * p + N] = jnp.where(big, thin, home[k])
 
-    for copy in x_peer + h_peer + a_peer + [above, l_near, l_far] + core_copy + home_copy:
+    for copy in x_peer + f_peer + h_peer + a_peer + [above, l_near, l_far] + core_copy + home_copy:
         copy.wait_send()
     for copy in side_copy + across_copy:
         copy.wait_send()
@@ -531,7 +553,8 @@
             buf(2 * N, N),
             buf(N, 2 * N),
             buf(G8, 48, 2 * N),
-            buf(G8, 16, 3 * N),
+            buf(G8, 16, 2 * N),
+            buf(G8, 16, N),
             buf(G8, 48, N),
             buf(2, N, N),
             buf(2, N, N),
@@ -555,8 +578,8 @@
             buf(5, 48, N),
             buf(5, 48, N),
             buf(3, 48, N),
-            DMA((28,)),
-            DMA((28,)),
+            DMA((35,)),
+            DMA((35,)),
             DMA((11,)),
             DMA((11,)),
             DMA((18,)),

time: 128 us -> 128 us (level)
  no operation moved by 1% of the time
where the time goes in v3:
time: 128 us; the launch traced here: 127 us
  Pallas kernels  124 us (97%)
  local copies, waits for them, and re-layouts  2.64 us (2%)
    pallas_call x1, Pallas kernels, local(): pl.pallas_call(sweep_kernel, out_shape=(jax.ShapeDtypeStruct((1, 2, N, N)...  124 us
    unnamed x4, local copies, waits for them, and re-layouts  2.64 us

profile of v3, /device:TPU:1, one launch (start us, length us, event | category | flops | bytes accessed | tf_op | source)
XLA Modules:
  0.0 127.1 jit_solution(7117568722916606210)
XLA Ops:
  0.6 123.8 %sweep.1 = (bf16[1,2,384,384]{3,2,1,0:T(8,128)(2,1)}, bf16[1,48,1536]{2,1,0:T(8,128)(2,1)}) custom-call(s32[16]{0:T(128)} %sizes.1, f32[2,4,4,16]{3,2,1,0:T(4,128)} %bitcast.2, s32[2,16]{1,0:T(2,128)} %bitcast.3, bf16[1,48,1536]{2,1,0:T(8,128)(2,1)} %rows3.1, bf16[2,384,384]{2,1,0:T(8,128)(2,1)} %bound_hbm.1, bf16[1,2,384,384]{3,2,1,0:T(8,128)(2,1)} %left4.1), custom_call_target="tpu_custom_call" | custom-call | tf_op jit(solution)/shard_map/sweep/pallas_call | solution.py:541
  124.4 0.0 copy-start
  124.4 2.0 %copy.10 = bf16[1,2,384,384]{3,2,1,0:T(8,128)(2,1)} copy(bf16[1,2,384,384]{3,2,1,0:T(8,128)(2,1)} %get-tuple-element.4) | data formatting | bytes 1179648
  126.4 0.0 copy-done
  126.4 0.7 copy.11
Async XLA Ops:
  124.4 2.0 %copy-start = (bf16[1,48,1536]{2,1,0:T(8,128)(2,1)S(1)}, bf16[1,48,1536]{2,1,0:T(8,128)(2,1)}, u32[]{:S(2)}) copy-start(bf16[1,48,1536]{2,1,0:T(8,128)(2,1)} %get-tuple-element.5) | copy-start | bytes 442372

commit v4 on v3

--- a/solution.py
+++ b/solution.py
@@ -21,10 +21,6 @@
 
 def mm_t(a, b):
     return lax.dot_general(a, b, (((1,), (1,)), ((), ())), preferred_element_type=F32)
-
-
-def t_mm(a, b):
-    return lax.dot_general(a, b, (((0,), (0,)), ((), ())), preferred_element_type=F32)
 
 
 def mix(coef, prods, target):
@@ -42,6 +38,10 @@
 
 def widen(tile):
     return jnp.concatenate([tile, jnp.zeros((T - H, T), BF)], axis=0)
+
+
+def widen_wide(tile):
+    return jnp.concatenate([tile, jnp.zeros((T - H, N), BF)], axis=0)
 
 
 def pull_near(coef, pull, base, m1):
@@ -112,7 +112,7 @@
 def sweep_kernel(
     sizes, ops, mask, rows3, bound_hbm, left4, env4, grads3,
     bound, left, near_acc, acol, pull, xs, hn, hf, ab, right, c0, m1, m3, got0, got1, got3, at1, at3, near_l, far_l,
-    mx0, mxh, mx_pull, parts, part_in, sums, sums_in, mids, mids_in, totals, home,
+    mx0, mxh, mx_pull, left_t, near_t, far_t, parts, part_in, sums, sums_in, mids, mids_in, totals, home,
     send, recv, csend, crecv, gsend, grecv, own_sem,
 ):
     rows, left_hbm, env_out, grads_out = rows3.at[0], left4.at[0], env4.at[0], grads3.at[0]
@@ -266,6 +266,15 @@
             def _(w=w):
                 down0[w].start()
 
+    def turn(tile, out):
+        for w in range(2):
+            out[:, T * w : T * w + T] = jnp.transpose(widen_wide(tile[w]))
+
+    def turn_left():
+        left_in.wait()
+        for w in range(2):
+            left_t[:, N * w : N * w + N] = jnp.transpose(left[w])
+
     def finish_above():
         pass_on(ab, 14, [])
         for d in range(3):
@@ -314,6 +323,13 @@
         finish_above()
         l_near.wait_recv()
         l_far.start()
+        turn(near_l, near_t)
+        turn_left()
+
+    @pl.when(sect == 0)
+    def _():
+        l_far.wait_recv()
+        turn(far_l, far_t)
 
     @pl.when(sect == 2)
     def _():
@@ -337,7 +353,7 @@
     ]
     blend = mix(coef, far_p, 3)
     for w in range(2):
-        mxh[w, 2] = blend[w]
+        mxh[2, w] = blend[w]
         far = mm_t(blend[w], acol[N + 2 * T : 2 * N, :])
         m3[w] = jnp.where(far_big, right[w, :H, :T], far[:H].astype(BF))
 
@@ -349,7 +365,7 @@
     def _():
         last3.start()
 
-    @pl.when(sect < 3)
+    @pl.when((sect > 0) & (sect < 3))
     def _():
         own_terms()
 
@@ -363,8 +379,8 @@
         near_p.append((None, both[:T], both[T:]))
     blend = [mix(coef, near_p, p) for p in (1, 2)]
     for w in range(2):
-        mxh[w, 0] = blend[0][w]
-        mxh[w, 1] = blend[1][w]
+        mxh[0, w] = blend[0][w]
+        mxh[1, w] = blend[1][w]
         near = mm_t(blend[0][w], acol[N : N + T, :]) + mm_t(blend[1][w], acol[N + T : N + 2 * T, :])
         m1[w] = jnp.where(near_big, right[w, :H, :T], near[:H].astype(BF))
 
@@ -429,23 +445,32 @@
         across_copy[k].wait_recv()
         totals[k] = (mids[k, half].astype(F32) + mids_in[k].astype(F32)).astype(BF)
 
-    left_in.wait()
-
     @pl.when(sect >= 2)
     def _():
+        turn_left()
         l_near.wait_recv()
         l_far.start()
-
-    l_far.wait_recv()
-    write_rows(parts.at[0], t_mm(far_l[0], mxh[0, 2, :H]) + t_mm(far_l[1], mxh[1, 2, :H]))
+        turn(near_l, near_t)
+
+    @pl.when(sect > 0)
+    def _():
+        l_far.wait_recv()
+        turn(far_l, far_t)
+
+    write_rows(parts.at[0], mm(far_t[...], mxh[2].reshape(2 * T, N)))
     core_copy[0].start()
     for p in (1, 2):
-        write_rows(parts.at[p], t_mm(near_l[0], mxh[0, p - 1, :H]) + t_mm(near_l[1], mxh[1, p - 1, :H]))
+        write_rows(parts.at[p], mm(near_t[...], mxh[p - 1].reshape(2 * T, N)))
         core_copy[p].start()
         if p == 1:
             add_core(0)
     add_core(1)
-    write_rows(parts.at[3], t_mm(left[0], mx0[0]) + t_mm(left[1], mx0[1]))
+
+    @pl.when(sect == 0)
+    def _():
+        own_terms()
+
+    write_rows(parts.at[3], mm(left_t[...], mx0[...].reshape(2 * N, N)))
     core_copy[3].start()
     add_side(0)
     add_core(2)
@@ -471,7 +496,7 @@
 
     mixed = pull_near(coef, pull, 0, at1)
     mixed.append(pull_far(coef, pull, 0, at3))
-    narrow = [t_mm(left[0], mixed[p][0]) + t_mm(left[1], mixed[p][1]) for p in range(3)]
+    narrow = [mm(left_t[...], jnp.concatenate(mixed[p], axis=0)) for p in range(3)]
     write_rows(parts.at[4], jnp.concatenate(narrow, axis=1))
     core_copy[4].start()
     add_side(3)
@@ -568,8 +593,11 @@
             buf(2, H, N),
             buf(2, H, N),
             buf(2, N, N),
-            buf(2, 3, T, N),
+            buf(3, 2, T, N),
             buf(2, 3, N, T),
+            buf(N, 2 * N),
+            buf(N, 2 * T),
+            buf(N, 2 * T),
             buf(5, G8, 48, N),
             buf(5, 4, 48, N),
             buf(5, 4, 48, N),
@@ -587,16 +615,14 @@
             DMA((6,)),
         ],
         compiler_params=pltpu.CompilerParams(
-            collective_id=0, has_side_effects=True, vmem_limit_bytes=64_000_000
+            collective_id=0, has_side_effects=True, vmem_limit_bytes=50_000_000
         ),
         name="sweep",
     )(
         sector_sizes,
         jnp.transpose(mpo_ops, (1, 2, 3, 0)),
         jnp.transpose(mpo_mask, (1, 0)),
-        site_tensor,
-        boundary_env,
-        left_env,
+        *[pltpu.with_memory_space_constraint(a, pltpu.HBM) for a in (site_tensor, boundary_env, left_env)],
     )
 
 

time: 128 us -> 125 us (0.977)
  Pallas kernels: 124 us -> 122 us
    pallas_call x1, Pallas kernels: 124 us -> 122 us  [local(): pl.pallas_call(sweep_kernel, out_shape=(jax.ShapeDtypeStruct((1, 2, N, N)...]
    unnamed x4 -> x8, local copies, waits for them, and re-layouts: 2.64 us -> 2.86 us
where the time goes in v4:
time: 125 us
  Pallas kernels  122 us (98%)
  local copies, waits for them, and re-layouts  2.86 us (2%)
    pallas_call x1, Pallas kernels, local(): pl.pallas_call(sweep_kernel, out_shape=(jax.ShapeDtypeStruct((1, 2, N, N)...  122 us
    unnamed x8, local copies, waits for them, and re-layouts  2.86 us

profile of v4, /device:TPU:1, one launch (start us, length us, event | category | flops | bytes accessed | tf_op | source)
XLA Modules:
  0.0 125.0 jit_solution(7263359327797098332)
XLA Ops:
  0.6 0.0 copy-start.1
  0.6 0.0 copy-start.2
  0.7 0.7 copy-done.1
  1.3 0.0 copy-done.2
  1.3 0.0 copy-start
  1.3 0.7 copy-done
  2.0 121.5 %sweep.1 = (bf16[1,2,384,384]{3,2,1,0:T(8,128)(2,1)S(1)}, bf16[1,48,1536]{2,1,0:T(8,128)(2,1)S(1)}) custom-call(s32[16]{0:T(128)S(1)} %copy-done.2, f32[2,4,4,16]{3,2,1,0:T(4,128)S(1)} %bitcast.2, s32[2,16]{1,0:T(2,128)S(1)} %bitcast.3, bf16[1,48,1536]{2,1,0:T(8,128)(2,1)} %rows3.1, bf16[2,384,384]{2,1,0:T(8,128)(2,1)} %bound_hbm.1, ...), custom_call_target="tpu_custom_call" | custom-call | tf_op jit(solution)/shard_map/sweep/pallas_call | solution.py:566
  123.6 0.8 copy.10
  124.4 0.7 copy.11
Async XLA Ops:
  0.6 0.7 copy-start.1
  0.6 0.7 copy-start.2
  1.3 0.7 copy-start

commit v5 on v4

--- a/solution.py
+++ b/solution.py
@@ -146,11 +146,11 @@
             for d in range(2):
                 pl.semaphore_signal(barrier, inc=1, device_id=goals[d][j], device_id_type=MESH)
 
-    own = [pltpu.make_async_copy(rows.at[:, pl.ds(0, N)], xs.at[within, :, pl.ds(0, N)], own_sem.at[0])]
+    own = [pltpu.make_async_copy(rows.at[:, pl.ds(0, N)], xs.at[within], own_sem.at[0])]
     for p in range(1, 4):
         own.append(
             pltpu.make_async_copy(
-                rows.at[:, pl.ds(N * p, T)], xs.at[within, :, pl.ds(N + T * (p - 1), T)], own_sem.at[p]
+                rows.at[:, pl.ds(N * p, T)], ab.at[within, :, pl.ds(T * (p - 1), T)], own_sem.at[p]
             )
         )
     for copy in own:
@@ -206,7 +206,9 @@
         copy.start()
     x_mate = [remote(xs.at[within], xs.at[within], sems, 10, mate)]
     x_mate[0].start()
-    above = remote(xs.at[within, :, pl.ds(N, N)], ab.at[within], sems, 6, (lower, blk))
+    above = remote(
+        ab.at[within, :, pl.ds(0, N)], ab.at[within, :, pl.ds(N, N)], sems, 6, (lower, blk)
+    )
     above.start()
     csems = (csend, crecv)
     l_near = remote(left_hbm.at[:, pl.ds(0, H), :], near_l, csems, 6, (sect, fore8))
@@ -232,7 +234,7 @@
     h_mate = [remote(hn.at[within], hn.at[within], sems, 24, mate)]
     for copy in h_peer + h_mate:
         copy.start()
-    landed(ab.at[within], 6)
+    landed(ab.at[within, :, pl.ds(N, N)], 6)
     a_peer = [remote(ab.at[within], ab.at[within], sems, 14 + d, peers[d]) for d in range(3)]
     a_mate = [remote(ab.at[within], ab.at[within], sems, 17, mate)]
     for copy in a_peer + a_mate:
@@ -281,15 +283,17 @@
             remote(ab.at[within], ab.at[within], sems, 18 + d, mate).wait()
         a_mate[0].wait()
         for w in range(G8):
-            line = lax.broadcasted_iota(jnp.int32, (48, N), 0) + 48 * w
-            pull[48 * w : 48 * w + 48, N:] = jnp.where(line < n_own, ab[w], jnp.zeros((48, N), BF))
+            line = lax.broadcasted_iota(jnp.int32, (48, 2 * N), 0) + 48 * w
+            pull[48 * w : 48 * w + 48, :] = jnp.where(
+                line < n_own, ab[w], jnp.zeros((48, 2 * N), BF)
+            )
 
     pass_on(xs, 7, x_mate)
     for copy in x_mate:
         copy.wait()
     for w in range(G8):
         line = lax.broadcasted_iota(jnp.int32, (48, N), 0) + 48 * w
-        acol[48 * w : 48 * w + 48, :] = jnp.where(line < n_own, xs[w, :, :N], jnp.zeros((48, N), BF))
+        acol[48 * w : 48 * w + 48, :] = jnp.where(line < n_own, xs[w], jnp.zeros((48, N), BF))
 
     @pl.when(sect == 3)
     def _():
@@ -406,9 +410,6 @@
     def _():
         finish_above()
 
-    for w in range(G8):
-        line = lax.broadcasted_iota(jnp.int32, (48, N), 0) + 48 * w
-        pull[48 * w : 48 * w + 48, :N] = jnp.where(line < n_own, xs[w, :, N:], jnp.zeros((48, N), BF))
 
     gsems = (gsend, grecv)
     core_copy = [
@@ -577,10 +578,10 @@
             pltpu.VMEM((2, N, N), F32),
             buf(2 * N, N),
             buf(N, 2 * N),
-            buf(G8, 48, 2 * N),
+            buf(G8, 48, N),
             buf(G8, 16, 2 * N),
             buf(G8, 16, N),
-            buf(G8, 48, N),
+            buf(G8, 48, 2 * N),
             buf(2, N, N),
             buf(2, N, N),
             buf(2, H, T),

time: 125 us -> 123 us (0.984); the launches traced: 125 us -> 121 us
  Pallas kernels: 122 us -> 118 us
    pallas_call x1, Pallas kernels: 122 us -> 118 us  [local(): pl.pallas_call(sweep_kernel, out_shape=(jax.ShapeDtypeStruct((1, 2, N, N)...]
where the time goes in v5:
time: 123 us; the launch traced here: 121 us
  Pallas kernels  118 us (96%)
  local copies, waits for them, and re-layouts  2.86 us (2%)
    pallas_call x1, Pallas kernels, local(): pl.pallas_call(sweep_kernel, out_shape=(jax.ShapeDtypeStruct((1, 2, N, N)...  118 us
    unnamed x8, local copies, waits for them, and re-layouts  2.86 us

profile of v5, /device:TPU:1, one launch (start us, length us, event | category | flops | bytes accessed | tf_op | source)
XLA Modules:
  0.0 121.4 jit_solution(14406293627588958623)
XLA Ops:
  0.6 0.0 copy-start.1
  0.6 0.0 copy-start.2
  0.7 0.7 copy-done.1
  1.3 0.0 copy-done.2
  1.3 0.0 copy-start
  1.3 0.7 copy-done
  2.0 117.9 %sweep.1 = (bf16[1,2,384,384]{3,2,1,0:T(8,128)(2,1)S(1)}, bf16[1,48,1536]{2,1,0:T(8,128)(2,1)S(1)}) custom-call(s32[16]{0:T(128)S(1)} %copy-done.2, f32[2,4,4,16]{3,2,1,0:T(4,128)S(1)} %bitcast.2, s32[2,16]{1,0:T(2,128)S(1)} %bitcast.3, bf16[1,48,1536]{2,1,0:T(8,128)(2,1)} %rows3.1, bf16[2,384,384]{2,1,0:T(8,128)(2,1)} %bound_hbm.1, ...), custom_call_target="tpu_custom_call" | custom-call | tf_op jit(solution)/shard_map/sweep/pallas_call | solution.py:567
  119.9 0.8 copy.10
  120.8 0.7 copy.11
Async XLA Ops:
  0.6 0.7 copy-start.1
  0.6 0.7 copy-start.2
  1.3 0.7 copy-start

commit v6 on v5

--- a/solution.py
+++ b/solution.py
@@ -326,7 +326,11 @@
         finish_near()
         finish_above()
         l_near.wait_recv()
-        l_far.start()
+
+        @pl.when(sect == 0)
+        def _():
+            l_far.start()
+
         turn(near_l, near_t)
         turn_left()
 
@@ -401,6 +405,10 @@
         up1.start()
         up3.start()
         back0.start()
+
+    @pl.when(sect == 1)
+    def _():
+        l_far.start()
 
     @pl.when(sect >= 2)
     def _():

time: 123 us -> 123 us (level)
  no operation moved by 1% of the time
where the time goes in v6:
time: 123 us; the launch traced here: 122 us
  Pallas kernels  118 us (96%)
  local copies, waits for them, and re-layouts  2.86 us (2%)
    pallas_call x1, Pallas kernels, local(): pl.pallas_call(sweep_kernel, out_shape=(jax.ShapeDtypeStruct((1, 2, N, N)...  118 us
    unnamed x8, local copies, waits for them, and re-layouts  2.86 us

profile of v6, /device:TPU:1, one launch (start us, length us, event | category | flops | bytes accessed | tf_op | source)
XLA Modules:
  0.0 122.0 jit_solution(1244560684161170603)
XLA Ops:
  0.6 0.0 copy-start.1
  0.6 0.0 copy-start.2
  0.7 0.7 copy-done.1
  1.3 0.0 copy-done.2
  1.3 0.0 copy-start
  1.3 0.7 copy-done
  2.0 118.4 %sweep.1 = (bf16[1,2,384,384]{3,2,1,0:T(8,128)(2,1)S(1)}, bf16[1,48,1536]{2,1,0:T(8,128)(2,1)S(1)}) custom-call(s32[16]{0:T(128)S(1)} %copy-done.2, f32[2,4,4,16]{3,2,1,0:T(4,128)S(1)} %bitcast.2, s32[2,16]{1,0:T(2,128)S(1)} %bitcast.3, bf16[1,48,1536]{2,1,0:T(8,128)(2,1)} %rows3.1, bf16[2,384,384]{2,1,0:T(8,128)(2,1)} %bound_hbm.1, ...), custom_call_target="tpu_custom_call" | custom-call | tf_op jit(solution)/shard_map/sweep/pallas_call | solution.py:575
  120.5 0.8 copy.10
  121.3 0.7 copy.11
Async XLA Ops:
  0.6 0.7 copy-start.1
  0.6 0.7 copy-start.2
  1.3 0.7 copy-start

commit v7 on v5

--- a/solution.py
+++ b/solution.py
@@ -110,8 +110,8 @@
 
 
 def sweep_kernel(
-    sizes, ops, mask, rows3, bound_hbm, left4, env4, grads3,
-    bound, left, near_acc, acol, pull, xs, hn, hf, ab, right, c0, m1, m3, got0, got1, got3, at1, at3, near_l, far_l,
+    sizes_hbm, ops_hbm, mask_hbm, rows3, bound_hbm, left4, env4, grads3,
+    sizes, ops, mask, bound, left, near_acc, acol, pull, xs, hn, hf, ab, right, c0, m1, m3, got0, got1, got3, at1, at3, near_l, far_l,
     mx0, mxh, mx_pull, left_t, near_t, far_t, parts, part_in, sums, sums_in, mids, mids_in, totals, home,
     send, recv, csend, crecv, gsend, grecv, own_sem,
 ):
@@ -157,9 +157,17 @@
         copy.start()
     bound_in = pltpu.make_async_copy(bound_hbm, bound, own_sem.at[4])
     left_in = pltpu.make_async_copy(left_hbm, left, own_sem.at[5])
+    small_in = [
+        pltpu.make_async_copy(src, dst, own_sem.at[6 + i])
+        for i, (src, dst) in enumerate(((sizes_hbm, sizes), (ops_hbm, ops), (mask_hbm, mask)))
+    ]
+    for copy in small_in:
+        copy.start()
     bound_in.start()
     left_in.start()
 
+    for copy in small_in:
+        copy.wait()
     n_own = sizes[sector]
     n_near = jnp.where(sector >= 1, sizes[jnp.maximum(sector - 1, 0)], 0)
     n_far = jnp.where(sector >= 2, sizes[jnp.maximum(sector - 2, 0)], 0)
@@ -352,6 +360,10 @@
             down0[w].wait_recv()
             settle(big, right, w, got0, got1, got3, near_acc[w], far_term(mixed, pull, N, w))
 
+    @pl.when((sect > 0) & (sect < 3))
+    def _():
+        own_terms()
+
     far_p = [
         (None, None, None, mm(acol[N + 2 * T : 2 * N, :], right[w]).astype(BF)) for w in range(2)
     ]
@@ -368,10 +380,6 @@
     @pl.when(sect == 0)
     def _():
         last3.start()
-
-    @pl.when((sect > 0) & (sect < 3))
-    def _():
-        own_terms()
 
     @pl.when(sect == 3)
     def _():
@@ -555,7 +563,6 @@
         up3.wait_send()
 
 
-SMEM = pl.BlockSpec(memory_space=pltpu.SMEM)
 VMEM = pl.BlockSpec(memory_space=pltpu.VMEM)
 HBM = pl.BlockSpec(memory_space=pltpu.HBM)
 
@@ -570,9 +577,12 @@
             jax.ShapeDtypeStruct((1, 2, N, N), BF),
             jax.ShapeDtypeStruct((1, 48, 4 * N), BF),
         ),
-        in_specs=[SMEM] * 3 + [HBM] * 3,
+        in_specs=[HBM] * 6,
         out_specs=(VMEM, VMEM),
         scratch_shapes=[
+            pltpu.SMEM((16,), jnp.int32),
+            pltpu.SMEM((2, 4, 4, 16), F32),
+            pltpu.SMEM((2, 16), jnp.int32),
             buf(2, N, N),
             buf(2, N, N),
             pltpu.VMEM((2, N, N), F32),
@@ -613,17 +623,24 @@
             DMA((11,)),
             DMA((18,)),
             DMA((18,)),
-            DMA((6,)),
+            DMA((9,)),
         ],
         compiler_params=pltpu.CompilerParams(
             collective_id=0, has_side_effects=True, vmem_limit_bytes=50_000_000
         ),
         name="sweep",
     )(
-        sector_sizes,
-        jnp.transpose(mpo_ops, (1, 2, 3, 0)),
-        jnp.transpose(mpo_mask, (1, 0)),
-        *[pltpu.with_memory_space_constraint(a, pltpu.HBM) for a in (site_tensor, boundary_env, left_env)],
+        *[
+            pltpu.with_memory_space_constraint(a, pltpu.HBM)
+            for a in (
+                sector_sizes,
+                jnp.transpose(mpo_ops, (1, 2, 3, 0)),
+                jnp.transpose(mpo_mask, (1, 0)),
+                site_tensor,
+                boundary_env,
+                left_env,
+            )
+        ]
     )
 
 

time: 123 us -> 120 us (0.976); the launches traced: 121 us -> 120 us
  local copies, waits for them, and re-layouts: 2.86 us -> 1.48 us
    unnamed x8 -> x2, local copies, waits for them, and re-layouts: 2.86 us -> 1.48 us
where the time goes in v7:
time: 120 us
  Pallas kernels  118 us (98%)
  local copies, waits for them, and re-layouts  1.48 us (1%)
    pallas_call x1, Pallas kernels, local(): pl.pallas_call(sweep_kernel, out_shape=(jax.ShapeDtypeStruct((1, 2, N, N)...  118 us

profile of v7, /device:TPU:1, one launch (start us, length us, event | category | flops | bytes accessed | tf_op | source)
XLA Modules:
  0.0 120.2 jit_solution(16448015903294035402)
XLA Ops:
  0.6 118.1 %sweep.1 = (bf16[1,2,384,384]{3,2,1,0:T(8,128)(2,1)S(1)}, bf16[1,48,1536]{2,1,0:T(8,128)(2,1)S(1)}) custom-call(s32[16]{0:T(128)} %sizes_hbm.1, f32[2,4,4,16]{3,2,1,0:T(4,128)} %bitcast.2, s32[2,16]{1,0:T(2,128)} %bitcast.3, bf16[1,48,1536]{2,1,0:T(8,128)(2,1)} %rows3.1, bf16[2,384,384]{2,1,0:T(8,128)(2,1)} %bound_hbm.1, bf16[1,2,384,384]{3,2,1,0:T(8,128)(2,1)} %left4.1), custom_call_target="tpu_custom_call" | custom-call | tf_op jit(solution)/shard_map/sweep/pallas_call | solution.py:574
  118.7 0.8 copy.10
  119.5 0.7 copy.11

commit v8 on v7

--- a/solution.py
+++ b/solution.py
@@ -265,6 +265,11 @@
     up1 = remote(got1, at1, csems, 9, (upper, blk))
     up3 = remote(got3, at3, csems, 10, (upper, blk))
 
+    gsems = (gsend, grecv)
+    core_copy = [
+        remote(parts.at[k, pl.ds((1 - core) * 4, 4)], part_in.at[k], gsems, k, mate) for k in range(5)
+    ]
+
     def own_terms():
         prods = [(mm(acol[:N, :], right[w]).astype(BF),) for w in range(2)]
         blend = mix(coef, prods, 0)
@@ -370,7 +375,21 @@
     blend = mix(coef, far_p, 3)
     for w in range(2):
         mxh[2, w] = blend[w]
-        far = mm_t(blend[w], acol[N + 2 * T : 2 * N, :])
+
+    def far_part():
+        write_rows(parts.at[0], mm(far_t[...], mxh[2].reshape(2 * T, N)))
+        core_copy[0].start()
+
+    def near_part(p):
+        write_rows(parts.at[p], mm(near_t[...], mxh[p - 1].reshape(2 * T, N)))
+        core_copy[p].start()
+
+    @pl.when(sect == 0)
+    def _():
+        far_part()
+
+    for w in range(2):
+        far = mm_t(mxh[2, w], acol[N + 2 * T : 2 * N, :])
         m3[w] = jnp.where(far_big, right[w, :H, :T], far[:H].astype(BF))
 
     @pl.when(sect > 0)
@@ -403,6 +422,8 @@
     @pl.when(sect == 0)
     def _():
         last1.start()
+        near_part(1)
+        near_part(2)
 
     @pl.when(sect < 3)
     def _():
@@ -419,10 +440,6 @@
         finish_above()
 
 
-    gsems = (gsend, grecv)
-    core_copy = [
-        remote(parts.at[k, pl.ds((1 - core) * 4, 4)], part_in.at[k], gsems, k, mate) for k in range(5)
-    ]
     odd, half = lax.rem(chip, 2), chip // 2
     side = (sect, base + (chip + 1 - 2 * odd) * 2 + core)
     across = (sect, base + lax.rem(chip + 2, 4) * 2 + core)
@@ -466,13 +483,13 @@
         l_far.wait_recv()
         turn(far_l, far_t)
 
-    write_rows(parts.at[0], mm(far_t[...], mxh[2].reshape(2 * T, N)))
-    core_copy[0].start()
-    for p in (1, 2):
-        write_rows(parts.at[p], mm(near_t[...], mxh[p - 1].reshape(2 * T, N)))
-        core_copy[p].start()
-        if p == 1:
-            add_core(0)
+    @pl.when(sect > 0)
+    def _():
+        far_part()
+        near_part(1)
+        near_part(2)
+
+    add_core(0)
     add_core(1)
 
     @pl.when(sect == 0)

time: 120 us -> 121 us (level)
  no operation moved by 1% of the time
where the time goes in v8:
time: 121 us
  Pallas kernels  118 us (98%)
  local copies, waits for them, and re-layouts  1.48 us (1%)
    pallas_call x1, Pallas kernels, local(): pl.pallas_call(sweep_kernel, out_shape=(jax.ShapeDtypeStruct((1, 2, N, N)...  118 us

profile of v8, /device:TPU:1, one launch (start us, length us, event | category | flops | bytes accessed | tf_op | source)
XLA Modules:
  0.0 120.6 jit_solution(9421094337792285383)
XLA Ops:
  0.6 118.5 %sweep.1 = (bf16[1,2,384,384]{3,2,1,0:T(8,128)(2,1)S(1)}, bf16[1,48,1536]{2,1,0:T(8,128)(2,1)S(1)}) custom-call(s32[16]{0:T(128)} %sizes_hbm.1, f32[2,4,4,16]{3,2,1,0:T(4,128)} %bitcast.2, s32[2,16]{1,0:T(2,128)} %bitcast.3, bf16[1,48,1536]{2,1,0:T(8,128)(2,1)} %rows3.1, bf16[2,384,384]{2,1,0:T(8,128)(2,1)} %bound_hbm.1, bf16[1,2,384,384]{3,2,1,0:T(8,128)(2,1)} %left4.1), custom_call_target="tpu_custom_call" | custom-call | tf_op jit(solution)/shard_map/sweep/pallas_call | solution.py:591
  119.1 0.8 copy.10
  119.9 0.7 copy.11
